TPU v7x, 32 devices: a whole 2x2x4 slice. The times are simulated.
32 devices in a mesh: dp: 2 (over x), row: 4 (over y, core), col: 4 (over z).
Axes of the slice: x: 2, y: 2, z: 4, core: 2. Of those that a mesh axis runs over, the one named last changes fastest.
Arguments:
- tokens: bfloat16 [5120, 2048], P(('dp', 'col'), 'row'), may hold values from -6 to 6
- cotangent: bfloat16 [5120, 2048], P(('dp', 'col'), 'row'), may hold values from -6 to 6
- seg_ids: int32 [5120], P('dp'), may hold values from 0 to 12, as said below
- positions: int32 [5120], P('dp'), may hold values from 0 to 1279, as said below
- parents: int32 [2, 13], P('dp'), may hold values from 0 to 4, as said below
- tree_sets: int32 [2], P('dp'), may hold values from 0 to 7
- gain_q: float32 [2048], P('col'), may hold values from 0.25 to 1.75
- gain_k: float32 [2048], P('col'), may hold values from 0.25 to 1.75
- gain_attn: float32 [2048], P('row'), may hold values from 0.25 to 1.75
- gain_ffn: float32 [2048], P('row'), may hold values from 0.25 to 1.75
- query_key_value_weight: bfloat16 [2048, 3, 2048], P('row', None, 'col'), may hold values from -0.125 to 0.125
- output_weight: bfloat16 [2048, 2048], P('col', 'row'), may hold values from -0.125 to 0.125
- gate_up_weight: bfloat16 [2048, 2, 8192], P('row', None, 'col'), may hold values from -0.125 to 0.125
- down_weight: bfloat16 [8192, 2048], P('col', 'row'), may hold values from -0.0625 to 0.0625
- query_key_value_adapter_first: float32 [3, 8, 16, 2048], P(None, None, None, 'row'), may hold values from -0.125 to 0.125
- query_key_value_adapter_second: float32 [3, 8, 16, 2048], P(None, None, None, 'col'), may hold values from -0.5 to 0.5
- output_adapter_first: float32 [8, 16, 2048], P(None, None, 'col'), may hold values from -0.125 to 0.125
- output_adapter_second: float32 [8, 16, 2048], P(None, None, 'row'), may hold values from -0.5 to 0.5
- gate_up_adapter_first: float32 [2, 8, 16, 2048], P(None, None, None, 'row'), may hold values from -0.125 to 0.125
- gate_up_adapter_second: float32 [2, 8, 16, 8192], P(None, None, None, 'col'), may hold values from -0.5 to 0.5
- down_adapter_first: float32 [8, 16, 8192], P(None, None, 'col'), may hold values from -0.0625 to 0.0625
- down_adapter_second: float32 [8, 16, 2048], P(None, None, 'row'), may hold values from -0.5 to 0.5
Outputs:
- layer_out: bfloat16 [5120, 2048], P(('dp', 'col'), 'row')
- input_grad: float32 [5120, 2048], P(('dp', 'col'), 'row')
- grad_a_qkv: float32 [3, 8, 16, 2048], P(None, 'dp', 'col', 'row')
- grad_b_qkv: float32 [3, 8, 16, 2048], P(None, 'dp', 'row', 'col')
- grad_a_out: float32 [8, 16, 2048], P('dp', 'row', 'col')
- grad_b_out: float32 [8, 16, 2048], P('dp', 'col', 'row')
- grad_a_gu: float32 [2, 8, 16, 2048], P(None, 'dp', 'col', 'row')
- grad_b_gu: float32 [2, 8, 16, 8192], P(None, 'dp', 'row', 'col')
- grad_a_down: float32 [8, 16, 8192], P('dp', 'row', 'col')
- grad_b_down: float32 [8, 16, 2048], P('dp', 'col', 'row')
Inputs may be any that keep to these rules, and one draw needn't show every extreme that they name: `seg_ids`: in each tree the first 1024 tokens are segment 0, the trunk; the other 12 segments of 128 tokens each follow in any order: branches are 1 to 4, leaves the higher numbers. The trunk's tokens have positions 0 to 1023 in order, a branch's 1024 onward, a leaf's 1024 + 128 onward. `parents`: the trunk and the branches have parent 0; each leaf has a branch as parent, and each branch has 2 leaves.
All inputs are finite; a program needn't handle non-finite values.
Results may differ from a plain program's by a relative error of at most 0.025.
Values may be sent and summed in bfloat16 or wider, within the bound.
A program may use at most 320 MiB of HBM per device.

v0:
```python
import jax
import jax.numpy as jnp
from jax import lax
from jax.sharding import PartitionSpec as P

D = 2048
HEAD = 128
RANK = 16
epsilon = 1e-06
rope_base = 500000.0
masked_out = -1e30
low = jnp.bfloat16
wide = jnp.float32
last_last = (((1,), (1,)), ((), ()))
first_first = (((0,), (0,)), ((), ()))


def dot(left, right):
    return jnp.dot(left, right, preferred_element_type=wide)


def dot_t(left, right):
    return lax.dot_general(left, right, last_last, preferred_element_type=wide)


def t_dot(left, right):
    return lax.dot_general(left, right, first_first, preferred_element_type=wide)


def angles(positions):
    half_width = HEAD // 2
    frequency = rope_base ** (-(jnp.arange(half_width, dtype=wide) * 2.0) / HEAD)
    angle_table = positions.astype(wide)[:, None] * frequency[None, :]
    return (jnp.cos(angle_table)[:, None, :], jnp.sin(angle_table)[:, None, :])


def rotate(values, cosine, sine):
    half_width = values.shape[-1] // 2
    first_half = values[..., :half_width]
    second_half = values[..., half_width:]
    return jnp.concatenate(
        [first_half * cosine - second_half * sine, second_half * cosine + first_half * sine],
        axis=-1,
    )


def norm_factor(square_sum):
    return lax.rsqrt(square_sum / D + epsilon)


def norm_back(scaled, flat, factor, cross_sum):
    return factor[:, None] * (scaled - flat * (cross_sum / D)[:, None])


def tree_mask(seg_ids, positions, parents):
    parent_row = parents[0]
    labels = jnp.arange(parent_row.shape[0], dtype=jnp.int32)
    parent_tok = jnp.sum(
        jnp.where(seg_ids[:, None] == labels[None, :], parent_row[None, :], 0), axis=1
    )
    grand_tok = jnp.sum(
        jnp.where(parent_tok[:, None] == labels[None, :], parent_row[None, :], 0), axis=1
    )
    on_path = (
        (seg_ids[None, :] == seg_ids[:, None])
        | (seg_ids[None, :] == parent_tok[:, None])
        | (seg_ids[None, :] == grand_tok[:, None])
    )
    return on_path & (positions[None, :] <= positions[:, None])


def per_device(
    tokens,
    cotangent,
    seg_ids,
    positions,
    parents,
    tree_sets,
    gain_q,
    gain_k,
    gain_attn,
    gain_ffn,
    query_key_value_weight,
    output_weight,
    gate_up_weight,
    down_weight,
    query_key_value_adapter_first,
    query_key_value_adapter_second,
    output_adapter_first,
    output_adapter_second,
    gate_up_adapter_first,
    gate_up_adapter_second,
    down_adapter_first,
    down_adapter_second,
):
    dp_count = lax.axis_size("dp")
    row_count = lax.axis_size("row")
    col_count = lax.axis_size("col")
    row_at = lax.axis_index("row")
    tree_tokens = seg_ids.shape[0]
    assert tree_sets.shape[0] == 1
    set_count = output_adapter_first.shape[0]
    own = tokens.shape[0] // row_count
    group = own * col_count
    width_row = tokens.shape[1]
    width_col = gain_q.shape[0]
    hidden_col = down_weight.shape[0]
    heads_col = width_col // HEAD
    score_scale = HEAD ** (-0.5)
    tree_set = tree_sets[0]

    def pick(table, axis):
        return lax.dynamic_index_in_dim(table, tree_set, axis, keepdims=False)

    narrow = jnp.concatenate(
        [
            pick(query_key_value_adapter_first, 1),
            pick(gate_up_adapter_first, 1),
            pick(output_adapter_second, 0)[None],
            pick(down_adapter_second, 0)[None],
        ],
        axis=0,
    ).astype(low)
    narrow_all = lax.all_gather(narrow, "row", axis=2, tiled=True)
    a_qkv = narrow_all[:3].reshape(3 * RANK, D)
    a_gu = narrow_all[3:5].reshape(2 * RANK, D)
    b_out = narrow_all[5]
    b_down = narrow_all[6]
    b_qkv = pick(query_key_value_adapter_second, 1).astype(low)
    b_gu = pick(gate_up_adapter_second, 1).astype(low)
    a_out = pick(output_adapter_first, 0).astype(low)
    a_down = pick(down_adapter_first, 0).astype(low)
    gains = lax.all_gather(jnp.stack([gain_attn, gain_ffn]), "row", axis=1, tiled=True)
    w_qkv = lax.all_gather(query_key_value_weight, "row", axis=0, tiled=True).reshape(
        D, 3 * width_col
    )
    w_out = lax.all_gather(output_weight, "row", axis=1, tiled=True)
    w_gu = lax.all_gather(gate_up_weight, "row", axis=0, tiled=True).reshape(D, 2 * hidden_col)
    w_down = lax.all_gather(down_weight, "row", axis=1, tiled=True)

    def to_tokens(values):
        return lax.all_to_all(values, "row", split_axis=0, concat_axis=1, tiled=True)

    def to_width(values):
        return lax.all_to_all(values, "row", split_axis=1, concat_axis=0, tiled=True)

    def gather_col(values):
        return lax.all_gather(values, "col", axis=0, tiled=True)

    def scatter_col(values):
        return lax.psum_scatter(values.astype(low), "col", scatter_dimension=0, tiled=True).astype(
            wide
        )

    def to_heads(values, parts):
        by_head = (
            values.reshape(group, parts, heads_col, HEAD)
            .transpose(2, 0, 1, 3)
            .reshape(heads_col, group, parts * HEAD)
        )
        moved = lax.all_to_all(by_head, "row", split_axis=0, concat_axis=0, tiled=True)
        return (
            moved.reshape(row_count, col_count, own, parts * HEAD)
            .transpose(1, 0, 2, 3)
            .reshape(tree_tokens, parts * HEAD)
        )

    def from_heads(values, parts):
        by_row = (
            values.reshape(col_count, row_count, own, parts * HEAD)
            .transpose(1, 0, 2, 3)
            .reshape(row_count, group, parts * HEAD)
        )
        moved = lax.all_to_all(by_row, "row", split_axis=0, concat_axis=0, tiled=True)
        return (
            moved.reshape(heads_col, group, parts, HEAD)
            .transpose(1, 2, 0, 3)
            .reshape(group, parts * width_col)
        )

    x_own = to_tokens(tokens)
    x = gather_col(x_own)
    red_qkv = dot_t(x, a_qkv).astype(low)
    raw = dot(x, w_qkv)
    extra = jnp.concatenate(
        [dot(red_qkv[:, RANK * j : RANK * (j + 1)], b_qkv[j]) for j in range(3)], axis=1
    )
    raw = raw + extra
    q_raw = raw[:, :width_col]
    k_raw = raw[:, width_col : 2 * width_col]
    v_raw = raw[:, 2 * width_col :]
    square_qk = lax.psum(
        jnp.stack([jnp.sum(q_raw * q_raw, axis=1), jnp.sum(k_raw * k_raw, axis=1)]), "col"
    )
    q_factor = norm_factor(square_qk[0])
    k_factor = norm_factor(square_qk[1])
    q_flat = q_raw * q_factor[:, None]
    k_flat = k_raw * k_factor[:, None]
    pos_own = lax.dynamic_index_in_dim(
        positions.reshape(col_count, row_count, own), row_at, 1, keepdims=False
    ).reshape(group)
    cos_own, sin_own = angles(pos_own)

    def turn(values, sine):
        return rotate(values.reshape(group, heads_col, HEAD), cos_own, sine).reshape(
            group, width_col
        )

    q_low = turn(q_flat * gain_q, sin_own).astype(low)
    k_low = turn(k_flat * gain_k, sin_own).astype(low)
    qkv_head = to_heads(jnp.concatenate([q_low, k_low, v_raw.astype(low)], axis=1), 3)
    q_head = qkv_head[:, :HEAD]
    k_head = qkv_head[:, HEAD : 2 * HEAD]
    v_head = qkv_head[:, 2 * HEAD :]
    visible = tree_mask(seg_ids, positions, parents)
    scores = jnp.where(visible, dot_t(q_head, k_head) * score_scale, masked_out)
    highest = jnp.max(scores, axis=1, keepdims=True)
    raised = jnp.exp(scores - highest)
    probs = raised / jnp.sum(raised, axis=1, keepdims=True)
    probs_low = probs.astype(low)
    attn_head = dot(probs_low, v_head).astype(low)
    attn = from_heads(attn_head, 1)
    red_out = dot_t(attn, a_out).astype(low)
    a_raw = scatter_col(dot(attn, w_out) + dot(red_out, b_out))
    a_factor = norm_factor(jnp.sum(a_raw * a_raw, axis=1))
    a_flat = a_raw * a_factor[:, None]
    h_own = x_own.astype(wide) + a_flat * gains[0]
    h = gather_col(h_own.astype(low))
    red_gu = dot_t(h, a_gu).astype(low)
    gate = dot(h, w_gu[:, :hidden_col]) + dot(red_gu[:, :RANK], b_gu[0])
    up = dot(h, w_gu[:, hidden_col:]) + dot(red_gu[:, RANK:], b_gu[1])
    sigma = jax.nn.sigmoid(gate)
    hidden = (gate * sigma * up).astype(low)
    red_down = dot_t(hidden, a_down).astype(low)
    f_raw = scatter_col(dot(hidden, w_down) + dot(red_down, b_down))
    f_factor = norm_factor(jnp.sum(f_raw * f_raw, axis=1))
    f_flat = f_raw * f_factor[:, None]
    out_own = (h_own + f_flat * gains[1]).astype(low)
    layer_out = to_width(out_own)
    g_own = to_tokens(cotangent).astype(wide)
    scaled_f = g_own * gains[1]
    d_f_own = norm_back(scaled_f, f_flat, f_factor, jnp.sum(scaled_f * f_flat, axis=1)).astype(low)
    d_f = gather_col(d_f_own)
    back_down = dot_t(d_f, b_down).astype(low)
    d_hidden = dot_t(d_f, w_down) + dot(back_down, a_down)
    d_gate = (d_hidden * up * sigma * (1.0 + gate * (1.0 - sigma))).astype(low)
    d_up = (d_hidden * (gate * sigma)).astype(low)
    back_gate = dot_t(d_gate, b_gu[0]).astype(low)
    back_up = dot_t(d_up, b_gu[1]).astype(low)
    back_gu = jnp.concatenate([back_gate, back_up], axis=1)
    d_h = g_own + scatter_col(
        dot_t(d_gate, w_gu[:, :hidden_col]) + dot_t(d_up, w_gu[:, hidden_col:]) + dot(back_gu, a_gu)
    )
    scaled_a = d_h * gains[0]
    d_a_own = norm_back(scaled_a, a_flat, a_factor, jnp.sum(scaled_a * a_flat, axis=1)).astype(low)
    d_a = gather_col(d_a_own)
    back_out = dot_t(d_a, b_out).astype(low)
    d_attn = (dot_t(d_a, w_out) + dot(back_out, a_out)).astype(low)
    d_attn_head = to_heads(d_attn, 1)
    d_probs = dot_t(d_attn_head, v_head)
    inner = jnp.sum(probs * d_probs, axis=1, keepdims=True)
    d_scores = (probs * (d_probs - inner)).astype(low)
    dq_head = (dot(d_scores, k_head) * score_scale).astype(low)
    dk_head = (t_dot(d_scores, q_head) * score_scale).astype(low)
    dv_head = t_dot(probs_low, d_attn_head).astype(low)
    d_qkv = from_heads(jnp.concatenate([dq_head, dk_head, dv_head], axis=1), 3)
    dq_n = turn(d_qkv[:, :width_col].astype(wide), -sin_own) * gain_q
    dk_n = turn(d_qkv[:, width_col : 2 * width_col].astype(wide), -sin_own) * gain_k
    cross_qk = lax.psum(
        jnp.stack([jnp.sum(dq_n * q_flat, axis=1), jnp.sum(dk_n * k_flat, axis=1)]), "col"
    )
    d_q = norm_back(dq_n, q_flat, q_factor, cross_qk[0]).astype(low)
    d_k = norm_back(dk_n, k_flat, k_factor, cross_qk[1]).astype(low)
    d_v = d_qkv[:, 2 * width_col :]
    d_raw = jnp.concatenate([d_q, d_k, d_v], axis=1)
    back_qkv = jnp.concatenate(
        [dot_t(d, b) for d, b in zip((d_q, d_k, d_v), (b_qkv[0], b_qkv[1], b_qkv[2]))], axis=1
    ).astype(low)
    in_own = d_h + scatter_col(dot_t(d_raw, w_qkv) + dot(back_qkv, a_qkv))
    input_grad = to_width(in_own.astype(low)).astype(wide)
    full_width = jnp.concatenate(
        [t_dot(back_qkv, x), t_dot(back_gu, h), t_dot(red_out, d_a), t_dot(red_down, d_f)], axis=0
    ).astype(low)
    full_width = lax.psum_scatter(full_width, "row", scatter_dimension=1, tiled=True)
    full_width = full_width.reshape(7, col_count, RANK // col_count, width_row).transpose(
        1, 0, 2, 3
    )
    full_width = lax.psum_scatter(full_width, "col", scatter_dimension=0, tiled=False)
    col_width = jnp.concatenate(
        [t_dot(red_qkv[:, RANK * j : RANK * (j + 1)], d) for j, d in enumerate((d_q, d_k, d_v))]
        + [
            t_dot(back_out, attn),
            t_dot(red_gu[:, :RANK], d_gate),
            t_dot(red_gu[:, RANK:], d_up),
            t_dot(back_down, hidden),
        ],
        axis=1,
    ).astype(low)
    col_width = lax.psum_scatter(col_width, "row", scatter_dimension=0, tiled=True)
    onehot = (tree_set == jnp.arange(set_count, dtype=jnp.int32)).astype(wide)
    owner = jnp.concatenate([full_width.reshape(-1), col_width.reshape(-1)])
    owner_all = lax.all_gather(owner, "dp", axis=0, tiled=False).astype(wide)
    onehot_all = lax.all_gather(onehot, "dp", axis=0, tiled=False)
    sets_own = set_count // dp_count
    onehot_own = lax.dynamic_slice_in_dim(onehot_all, lax.axis_index("dp") * sets_own, sets_own, 1)
    per_set = jnp.sum(onehot_own[:, :, None] * owner_all[:, None, :], axis=0)
    split_at = full_width.size
    full_sets = per_set[:, :split_at].reshape(sets_own, 7, RANK // col_count, width_row)
    col_sets = per_set[:, split_at:].reshape(sets_own, RANK // row_count, -1)
    grad_a_qkv = full_sets[:, :3].transpose(1, 0, 2, 3)
    grad_a_gu = full_sets[:, 3:5].transpose(1, 0, 2, 3)
    grad_b_out = full_sets[:, 5]
    grad_b_down = full_sets[:, 6]
    grad_b_qkv = jnp.stack([col_sets[..., width_col * j : width_col * (j + 1)] for j in range(3)])
    grad_a_out = col_sets[..., 3 * width_col : 4 * width_col]
    gu_at = 4 * width_col
    grad_b_gu = jnp.stack(
        [col_sets[..., gu_at + hidden_col * j : gu_at + hidden_col * (j + 1)] for j in range(2)]
    )
    grad_a_down = col_sets[..., gu_at + 2 * hidden_col :]
    return (
        layer_out,
        input_grad,
        grad_a_qkv,
        grad_b_qkv,
        grad_a_out,
        grad_b_out,
        grad_a_gu,
        grad_b_gu,
        grad_a_down,
        grad_b_down,
    )


def solution(mesh):
    in_specs = (
        P(("dp", "col"), "row"),
        P(("dp", "col"), "row"),
        P("dp"),
        P("dp"),
        P("dp", None),
        P("dp"),
        P("col"),
        P("col"),
        P("row"),
        P("row"),
        P("row", None, "col"),
        P("col", "row"),
        P("row", None, "col"),
        P("col", "row"),
        P(None, None, None, "row"),
        P(None, None, None, "col"),
        P(None, None, "col"),
        P(None, None, "row"),
        P(None, None, None, "row"),
        P(None, None, None, "col"),
        P(None, None, "col"),
        P(None, None, "row"),
    )
    out_specs = (
        P(("dp", "col"), "row"),
        P(("dp", "col"), "row"),
        P(None, "dp", "col", "row"),
        P(None, "dp", "row", "col"),
        P("dp", "row", "col"),
        P("dp", "col", "row"),
        P(None, "dp", "col", "row"),
        P(None, "dp", "row", "col"),
        P("dp", "row", "col"),
        P("dp", "col", "row"),
    )
    return jax.shard_map(
        per_device, mesh=mesh, in_specs=in_specs, out_specs=out_specs, check_vma=False
    )
```

profile of v0, /device:TPU:0, one launch (start us, length us, event | category | flops | bytes accessed | tf_op | source)
XLA Modules:
  0.0 1157.8 jit_solution(14469267757178420043)
XLA Ops:
  7.2 14.6 %all_to_all.84 = bf16[4,160,512]{2,1,0:T(8,128)(2,1)S(1)} all-to-all(bf16[4,160,512]{2,1,0:T(8,128)(2,1)} %bitcast.270), channel_id=1, replica_groups=mesh['dp'=2,'row'=4,'col'=4] {'row'}, dimensions={0} | all-to-all | bytes 1310720 | tf_op jit(solution)/shard_map/all_to_all | solution.py:142
  39.2 39.6 %all-gather.11.cloned.1.call-done = bf16[640,2048]{1,0:T(8,128)(2,1)} async-done(((bf16[160,2048]{1,0:T(8,128)(2,1)}), bf16[640,2048]{1,0:T(8,128)(2,1)}) %all-gather.11.cloned.1.call-update) | async-done | bytes 2621456 | tf_op jit(solution)/shard_map/all_gather | solution.py:148
  84.6 40.9 %all-gather.13.cloned.1.call-done = bf16[2048,3,512]{0,2,1:T(8,128)(2,1)} async-done(((bf16[512,3,512]{0,2,1:T(8,128)(2,1)}), bf16[2048,3,512]{0,2,1:T(8,128)(2,1)}) %all-gather.13.cloned.1.call-update) | async-done | bytes 6291472 | tf_op jit(solution)/shard_map/all_gather | solution.py:134
  137.0 12.3 %psum.14 = f32[2,640]{1,0:T(2,128)S(1)} all-reduce(f32[2,640]{1,0:T(2,128)S(1)} %pad_maximum_fusion.17), channel_id=1, replica_groups=mesh['dp'=2,'row'=4,'col'=4] {'col'}, use_global_device_ids=true, to_apply=%region_4.5 | all-reduce | flops 1280 | bytes 10240 | tf_op jit(solution)/shard_map/psum | solution.py:192
  179.6 34.4 %all-to-all-done.1 = bf16[4,640,384]{1,2,0:T(8,128)(2,1)} async-done(((bf16[4,640,384]{1,2,0:T(8,128)(2,1)}), bf16[4,640,384]{1,2,0:T(8,128)(2,1)}, u32[]{:S(2)}, u32[]{:S(2)}) %all-to-all-start.1) | async-done | bytes 1966112 | tf_op jit(solution)/shard_map/all_to_all | solution.py:161
  228.3 8.6 copy-done.2
  240.8 10.9 fusion.15
  251.8 12.7 %all_to_all.85 = bf16[4,640,128]{2,1,0:T(8,128)(2,1)S(1)} all-to-all(bf16[4,640,128]{2,1,0:T(8,128)(2,1)S(1)} %bitcast.254), channel_id=1, replica_groups=mesh['dp'=2,'row'=4,'col'=4] {'row'}, dimensions={0} | all-to-all | bytes 1310720 | tf_op jit(solution)/shard_map/all_to_all | solution.py:174
  278.0 43.6 %reduce-scatter.7.cloned.1.call-done = bf16[160,2048]{1,0:T(8,128)(2,1)} async-done(((bf16[640,2048]{1,0:T(8,128)(2,1)}), bf16[160,2048]{1,0:T(8,128)(2,1)}) %reduce-scatter.7.cloned.1.call-update) | async-done | bytes 655376 | tf_op jit(solution)/shard_map/reduce_scatter | solution.py:151
  327.8 52.1 %all-gather.17.cloned.1.call-done = bf16[640,2048]{1,0:T(8,128)(2,1)} async-done(((bf16[160,2048]{1,0:T(8,128)(2,1)}), bf16[640,2048]{1,0:T(8,128)(2,1)}) %all-gather.17.cloned.1.call-update) | async-done | bytes 2621456 | tf_op jit(solution)/shard_map/all_gather | solution.py:148
  382.5 103.5 %all-gather.19.cloned.1.call-done = bf16[2048,2,2048]{2,1,0:T(2,128)(2,1)} async-done(((bf16[512,2,2048]{2,1,0:T(2,128)(2,1)}), bf16[2048,2,2048]{2,1,0:T(2,128)(2,1)}) %all-gather.19.cloned.1.call-update) | async-done | bytes 16777232 | tf_op jit(solution)/shard_map/all_gather | solution.py:138
  486.0 13.0 %copy.133 = bf16[256,8,2,2048]{3,1,2,0:T(8,128)(2,1)S(1)} copy(bf16[256,8,2,2048]{3,2,1,0:T(2,128)(2,1)} %bitcast.231) | data formatting | bytes 33554432
  525.4 20.5 %all-gather.21.cloned.1.call-done = bf16[2048,2048]{1,0:T(8,128)(2,1)} async-done(((bf16[2048,512]{1,0:T(8,128)(2,1)}), bf16[2048,2048]{1,0:T(8,128)(2,1)}) %all-gather.21.cloned.1.call-update) | async-done | bytes 8388624 | tf_op jit(solution)/shard_map/all_gather | solution.py:139
  545.9 8.8 fusion.116
  559.0 12.6 %all_to_all.86 = bf16[4,160,512]{2,1,0:T(8,128)(2,1)S(1)} all-to-all(bf16[4,160,512]{2,1,0:T(8,128)(2,1)S(1)} %bitcast.271), channel_id=1, replica_groups=mesh['dp'=2,'row'=4,'col'=4] {'row'}, dimensions={0} | all-to-all | bytes 1310720 | tf_op jit(solution)/shard_map/all_to_all | solution.py:142
  571.9 38.2 %reduce-scatter.9.cloned.1.call-done = bf16[160,2048]{1,0:T(8,128)(2,1)} async-done(((bf16[640,2048]{1,0:T(8,128)(2,1)}), bf16[160,2048]{1,0:T(8,128)(2,1)}) %reduce-scatter.9.cloned.1.call-update) | async-done | bytes 655376 | tf_op jit(solution)/shard_map/reduce_scatter | solution.py:151
  614.8 54.1 %all-gather.23.cloned.1.call-done = bf16[640,2048]{1,0:T(8,128)(2,1)} async-done(((bf16[160,2048]{1,0:T(8,128)(2,1)}), bf16[640,2048]{1,0:T(8,128)(2,1)}) %all-gather.23.cloned.1.call-update) | async-done | bytes 2621456 | tf_op jit(solution)/shard_map/all_gather | solution.py:148
  668.9 11.2 fusion.117
  681.9 9.8 multiply_convert_fusion.1
  716.6 51.0 %reduce-scatter.11.cloned.1.call-done = bf16[160,2048]{1,0:T(8,128)(2,1)} async-done(((bf16[640,2048]{1,0:T(8,128)(2,1)}), bf16[160,2048]{1,0:T(8,128)(2,1)}) %reduce-scatter.11.cloned.1.call-update) | async-done | bytes 655376 | tf_op jit(solution)/shard_map/reduce_scatter | solution.py:151
  772.2 54.6 %all-gather.25.cloned.1.call-done = bf16[640,2048]{1,0:T(8,128)(2,1)} async-done(((bf16[160,2048]{1,0:T(8,128)(2,1)}), bf16[640,2048]{1,0:T(8,128)(2,1)}) %all-gather.25.cloned.1.call-update) | async-done | bytes 2621456 | tf_op jit(solution)/shard_map/all_gather | solution.py:148
  834.3 12.8 %all_to_all.87 = bf16[4,640,128]{2,1,0:T(8,128)(2,1)S(1)} all-to-all(bf16[4,640,128]{2,1,0:T(8,128)(2,1)S(1)} %bitcast.256), channel_id=1, replica_groups=mesh['dp'=2,'row'=4,'col'=4] {'row'}, dimensions={0} | all-to-all | bytes 1310720 | tf_op jit(solution)/shard_map/all_to_all | solution.py:161
  847.2 11.3 fusion.20
  858.5 20.5 %multiply_reduce_fusion = (f32[2560]{0:T(1024)S(1)}, f32[2560,2560]{0,1:T(8,128)}) fusion(f32[2560]{0:T(1024)S(1)} %copy-done.64, f32[2560,2560]{0,1:T(8,128)} %copy-done.2, f32[2560]{0:T(1024)S(1)} %copy-done.62, bf16[2560,128]{1,0:T(8,128)(2,1)S(1)} %bitcast.273, bf16[2560,384]{1,0:T(8,128)(2,1)S(1)} %bitcast.249), kind=kOutput, calls=%fused_computation.1 | convolution fusion | flops 1703933440 | bytes 53774336 | tf_op jit(solution)/shard_map/dot_general | solution.py:23
  878.9 22.4 %multiply_convert_fusion = bf16[2560,2560]{0,1:T(8,128)(2,1)} fusion(f32[2560,2560]{0,1:T(8,128)} %get-tuple-element.100, f32[2560]{0:T(1024)S(1)} %get-tuple-element.99, f32[2560]{0:T(1024)S(1)} %copy-done.64, f32[2560,2560]{0,1:T(8,128)} %copy-done.2, f32[2560]{0:T(1024)S(1)} %copy-done.62), kind=kLoop, calls=%fused_computation | loop fusion | flops 32768000 | bytes 65566720 | tf_op jit(solution)/shard_map/convert_element_type | solution.py:262
  901.3 9.1 fusion.18
  933.0 17.8 %all-to-all-done.6 = bf16[4,640,384]{2,1,0:T(8,128)(2,1)S(1)} async-done(((bf16[4,640,384]{2,1,0:T(8,128)(2,1)}), bf16[4,640,384]{2,1,0:T(8,128)(2,1)S(1)}, u32[]{:S(2)}, u32[]{:S(2)}) %all-to-all-start.6) | async-done | bytes 1966112 | tf_op jit(solution)/shard_map/all_to_all | solution.py:174
  971.6 9.6 psum.15
  993.5 8.8 fusion.26
  1028.9 12.6 %all-reduce.7.cloned.1.call-done = bf16[16,8192]{1,0:T(8,128)(2,1)} async-done(((bf16[16,8192]{1,0:T(8,128)(2,1)}), bf16[16,8192]{1,0:T(8,128)(2,1)}) %all-reduce.7.cloned.1.call-update) | async-done | bytes 262160
  1042.4 36.0 %all-reduce.5.cloned.1.call-done = bf16[4,7,4,512]{3,2,0,1:T(4,128)(2,1)} async-done(((bf16[4,7,4,512]{3,2,0,1:T(4,128)(2,1)}), bf16[4,7,4,512]{3,2,0,1:T(4,128)(2,1)}) %all-reduce.5.cloned.1.call-update) | async-done | bytes 114704
  1091.2 41.5 %reduce-scatter.13.cloned.1.call-done = bf16[160,2048]{1,0:T(8,128)(2,1)} async-done(((bf16[640,2048]{1,0:T(8,128)(2,1)}), bf16[160,2048]{1,0:T(8,128)(2,1)}) %reduce-scatter.13.cloned.1.call-update) | async-done | bytes 655376 | tf_op jit(solution)/shard_map/reduce_scatter | solution.py:151
  (348 shorter events, 291.6 us)
Async XLA Ops:
  7.2 320.6 %copy-start = (f32[2,8,16,2048]{3,2,1,0:T(8,128)S(1)}, f32[2,8,16,2048]{3,2,1,0:T(8,128)}, u32[]{:S(2)}) copy-start(f32[2,8,16,2048]{3,2,1,0:T(8,128)} %param.41) | copy-start | bytes 6291460
  7.2 71.5 %all-gather.11.cloned.1.call-start = ((), (), s32[]{:S(2)}) async-start(), calls=%async_computation.13 | async-start | bytes 3276800 | tf_op jit(solution)/shard_map/all_gather | solution.py:148
  22.8 102.7 %all-gather.13.cloned.1.call-start = ((), (), s32[]{:S(2)}) async-start(), calls=%async_computation.14 | async-start | bytes 7864320 | tf_op jit(solution)/shard_map/all_gather | solution.py:134
  36.0 46.7 %copy-start.34 = (bf16[3,16,2048]{2,1,0:T(8,128)(2,1)}, bf16[3,16,2048]{2,1,0:T(8,128)(2,1)S(1)}, u32[]{:S(2)}) copy-start(bf16[3,16,2048]{2,1,0:T(8,128)(2,1)S(1)} %slice.228) | copy-start | bytes 589828
  37.0 47.2 %copy-start.43 = (bf16[3,1,16,512]{3,2,1,0:T(8,128)(2,1)}, bf16[3,1,16,512]{3,2,1,0:T(8,128)(2,1)S(1)}, u32[]{:S(2)}) copy-start(bf16[3,1,16,512]{3,2,1,0:T(8,128)(2,1)S(1)} %dynamic-slice_convert_fusion.2) | copy-start | bytes 147460
  173.8 40.1 %all-to-all-start.1 = ((bf16[4,640,384]{1,2,0:T(8,128)(2,1)}), bf16[4,640,384]{1,2,0:T(8,128)(2,1)}, u32[]{:S(2)}, u32[]{:S(2)}) async-start(bf16[4,640,384]{1,2,0:T(8,128)(2,1)} %bitcast.242), calls=%async_computation.1 | async-start | bytes 3932160 | tf_op jit(solution)/shard_map/all_to_all | solution.py:161
  178.4 87.4 %all-gather.15.cloned.1.call-start = ((), (), s32[]{:S(2)}) async-start(), calls=%async_computation.15 | async-start | bytes 2621440 | tf_op jit(solution)/shard_map/all_gather | solution.py:137
  179.1 142.5 %reduce-scatter.7.cloned.1.call-start = ((), (), s32[]{:S(2)}) async-start(), calls=%async_computation.16 | async-start | bytes 3276800 | tf_op jit(solution)/shard_map/reduce_scatter | solution.py:151
  219.8 21.0 %copy-start.28 = (bf16[4,4,160,384]{3,2,1,0:T(8,128)(2,1)}, bf16[4,4,160,384]{3,2,1,0:T(8,128)(2,1)S(1)}, u32[]{:S(2)}) copy-start(bf16[4,4,160,384]{3,2,1,0:T(8,128)(2,1)S(1)} %copy.108) | copy-start | bytes 5898244
  272.1 50.8 %copy-start.20 = (bf16[4,20,8,512]{3,2,0,1:T(8,128)(2,1)S(1)}, bf16[4,20,8,512]{3,2,0,1:T(8,128)(2,1)}, u32[]{:S(2)}) copy-start(bf16[4,20,8,512]{3,2,0,1:T(8,128)(2,1)} %copy.129) | copy-start | bytes 1966084
  272.1 107.7 %all-gather.17.cloned.1.call-start = ((), (), s32[]{:S(2)}) async-start(), calls=%async_computation.17 | async-start | bytes 3276800 | tf_op jit(solution)/shard_map/all_gather | solution.py:148
  325.2 160.8 %all-gather.19.cloned.1.call-start = ((), (), s32[]{:S(2)}) async-start(), calls=%async_computation.18 | async-start | bytes 20971520 | tf_op jit(solution)/shard_map/all_gather | solution.py:138
  325.8 220.1 %all-gather.21.cloned.1.call-start = ((), (), s32[]{:S(2)}) async-start(), calls=%async_computation.19 | async-start | bytes 10485760 | tf_op jit(solution)/shard_map/all_gather | solution.py:139
  326.6 283.6 %reduce-scatter.9.cloned.1.call-start = ((), (), s32[]{:S(2)}) async-start(), calls=%async_computation.20 | async-start | bytes 3276800 | tf_op jit(solution)/shard_map/reduce_scatter | solution.py:151
  382.5 134.7 %copy-start.48 = (bf16[640,32]{0,1:T(8,128)(2,1)}, bf16[640,32]{0,1:T(8,128)(2,1)S(1)}, u32[]{:S(2)}) copy-start(bf16[640,32]{0,1:T(8,128)(2,1)S(1)} %convolution_convert_fusion.8) | copy-start | bytes 122884
  525.4 29.3 %copy-start.50 = (bf16[640,16]{0,1:T(8,128)(2,1)}, bf16[640,16]{0,1:T(8,128)(2,1)S(1)}, u32[]{:S(2)}) copy-start(bf16[640,16]{0,1:T(8,128)(2,1)S(1)} %convolution_convert_fusion.17) | copy-start | bytes 61444
  557.9 111.0 %all-gather.23.cloned.1.call-start = ((), (), s32[]{:S(2)}) async-start(), calls=%async_computation.21 | async-start | bytes 3276800 | tf_op jit(solution)/shard_map/all_gather | solution.py:148
  571.9 197.2 %copy-start.3 = (f32[4,20,8,512]{3,2,0,1:T(8,128)}, f32[4,20,8,512]{3,2,0,1:T(8,128)S(1)}, u32[]{:S(2)}) copy-start(f32[4,20,8,512]{3,2,0,1:T(8,128)S(1)} %copy.130) | copy-start | bytes 3932164
  614.3 153.3 %reduce-scatter.11.cloned.1.call-start = ((), (), s32[]{:S(2)}) async-start(), calls=%async_computation.22 | async-start | bytes 3276800 | tf_op jit(solution)/shard_map/reduce_scatter | solution.py:151
  716.5 51.1 %copy-start.21 = (bf16[160,2048]{1,0:T(8,128)(2,1)S(1)}, bf16[160,2048]{1,0:T(8,128)(2,1)}, u32[]{:S(2)}) copy-start(bf16[160,2048]{1,0:T(8,128)(2,1)} %reduce-scatter.7.cloned.1.call-done) | copy-start | bytes 1966084
  716.5 110.3 %all-gather.25.cloned.1.call-start = ((), (), s32[]{:S(2)}) async-start(), calls=%async_computation.23 | async-start | bytes 3276800 | tf_op jit(solution)/shard_map/all_gather | solution.py:148
  922.8 28.0 %all-to-all-start.6 = ((bf16[4,640,384]{2,1,0:T(8,128)(2,1)}), bf16[4,640,384]{2,1,0:T(8,128)(2,1)S(1)}, u32[]{:S(2)}, u32[]{:S(2)}) async-start(bf16[4,640,384]{2,1,0:T(8,128)(2,1)} %bitcast.243), calls=%async_computation.9 | async-start | bytes 3932160 | tf_op jit(solution)/shard_map/all_to_all | solution.py:174
  926.6 79.7 %reduce-scatter.15.cloned.1.call-start = ((), (), s32[]{:S(2)}) async-start(), calls=%async_computation.25 | async-start | bytes 573440 | tf_op jit(solution)/shard_map/reduce_scatter | solution.py:284
  987.2 54.2 %all-reduce.7.cloned.1.call-start = ((), (), s32[]{:S(2)}) async-start(), calls=%async_computation.27 | async-start | bytes 524288
  993.5 84.9 %all-reduce.5.cloned.1.call-start = ((), (), s32[]{:S(2)}) async-start(), calls=%async_computation.26 | async-start | bytes 229376
  1007.8 124.9 %reduce-scatter.13.cloned.1.call-start = ((), (), s32[]{:S(2)}) async-start(), calls=%async_computation.24 | async-start | bytes 3276800 | tf_op jit(solution)/shard_map/reduce_scatter | solution.py:151
  1014.8 14.1 %all-to-all-start.3 = ((bf16[160,4,512]{2,0,1:T(8,128)(2,1)}), bf16[160,4,512]{2,0,1:T(8,128)(2,1)S(1)}, u32[]{:S(2)}, u32[]{:S(2)}) async-start(bf16[160,4,512]{2,0,1:T(8,128)(2,1)} %bitcast.215), calls=%async_computation.5 | async-start | bytes 1310720 | tf_op jit(solution)/shard_map/all_to_all | solution.py:145
  1085.3 47.4 %copy-start.4 = (f32[4,20,8,512]{3,2,0,1:T(8,128)S(1)}, f32[4,20,8,512]{3,2,0,1:T(8,128)}, u32[]{:S(2)}) copy-start(f32[4,20,8,512]{3,2,0,1:T(8,128)} %copy-done.3) | copy-start | bytes 3932164
  1085.4 47.4 %copy-start.26 = (bf16[160,2048]{1,0:T(8,128)(2,1)S(1)}, bf16[160,2048]{1,0:T(8,128)(2,1)}, u32[]{:S(2)}) copy-start(bf16[160,2048]{1,0:T(8,128)(2,1)} %reduce-scatter.11.cloned.1.call-done) | copy-start | bytes 1966084
  1086.9 47.2 %copy-start.37 = (f32[4,7,4,512]{3,2,1,0:T(4,128)}, f32[4,7,4,512]{3,2,1,0:T(4,128)S(1)}, u32[]{:S(2)}) copy-start(f32[4,7,4,512]{3,2,1,0:T(4,128)S(1)} %reshape.348) | copy-start | bytes 688132
  1135.0 15.9 %copy-start.1 = (f32[2,8,16,2048]{3,2,1,0:T(8,128)S(1)}, f32[2,8,16,2048]{3,2,1,0:T(8,128)}, u32[]{:S(2)}) copy-start(f32[2,8,16,2048]{3,2,1,0:T(8,128)} %param.41) | copy-start | bytes 6291460
  1135.0 13.8 %all-to-all-start.7 = ((bf16[160,4,512]{2,0,1:T(8,128)(2,1)}), bf16[160,4,512]{2,0,1:T(8,128)(2,1)S(1)}, u32[]{:S(2)}, u32[]{:S(2)}) async-start(bf16[160,4,512]{2,0,1:T(8,128)(2,1)} %bitcast.214), calls=%async_computation.11 | async-start | bytes 1310720 | tf_op jit(solution)/shard_map/all_to_all | solution.py:145
  (67 other events, 376.3 us)
Sparse Core Ops, SparseCore 0:
  22.9 55.7 all-gather.10
  80.3 45.1 all-gather.12
  180.8 32.5 all-gather.14
  272.3 49.3 reduce-scatter.6
  325.3 54.4 all-gather.16
  381.3 104.6 all-gather.18
  487.6 58.2 all-gather.20
  558.1 52.0 reduce-scatter.8
  614.4 54.4 all-gather.22
  716.7 50.8 reduce-scatter.10
  772.3 54.4 all-gather.24
  987.4 18.8 reduce-scatter.14
  1009.1 32.2 all-reduce.6
  1044.3 34.0 all-reduce.4
  1080.6 52.0 reduce-scatter.12
where the time goes:
time: 1170 us; the launch traced here: 1160 us
  waiting for transfers between devices  654 us (56%)
  matrix products  212 us (18%)
  local copies, waits for them, and re-layouts  96.2 us (8%)
  blocking collectives  95.6 us (8%)
  other arithmetic  66.5 us (6%)
  starting transfers between devices  16.8 us (1%)
  between operations  16.8 us (1%)
    all_gather x4, waiting for transfers between devices, gather_col(): return lax.all_gather(values, 'col', axis=0, tiled=True)  200 us
    reduce_scatter x4, waiting for transfers between devices, scatter_col(): lax.psum_scatter(values.astype(low), 'col', scatter_dimension=0, tiled=True)  174 us
    all_gather x1, waiting for transfers between devices, per_device(): lax.all_gather(gate_up_weight, 'row', axis=0, tiled=True)  104 us
    dot_general x18, matrix products, dot(): return jnp.dot(left, right, preferred_element_type=wide)  93.1 us
    dot_general x18, matrix products, dot_t(): return lax.dot_general(left, right, last_last, preferred_element_type=wide)  84.5 us
    unnamed x17, waiting for transfers between devices  50.7 us
    unnamed x173, local copies, waits for them, and re-layouts  41 us
    all_gather x1, waiting for transfers between devices, per_device(): lax.all_gather(query_key_value_weight, 'row', axis=0, tiled=True)  40.9 us
  transfers between devices with their start and end apart: 19, of which 18 were waited for; matrix products, arithmetic and copies ran while one was open for 11% of the time, Pallas kernels for 0%

commit v1 on v0

--- a/solution.py
+++ b/solution.py
@@ -93,6 +93,22 @@
     down_adapter_first,
     down_adapter_second,
 ):
+
+    def begin_bands_by_axis(frame, device_axis="row"):
+        u_next = lax.axis_size(device_axis)
+        out_arr, carry = (u_next, lax.axis_index(device_axis))
+        aux, x_next = (frame, 1)
+        while x_next < out_arr:
+            n_now = range(out_arr)
+            finding = map(lambda hop_no: (hop_no, hop_no ^ x_next), n_now)
+            f_next = list(finding)
+            upper = lax.ppermute(aux, device_axis, f_next)
+            p_next = jnp.concatenate([aux, upper], axis=0)
+            inter = jnp.concatenate([upper, aux], axis=0)
+            aux = jnp.where(carry & x_next == 0, p_next, inter)
+            x_next = 2 * x_next
+        return aux
+
     dp_count = lax.axis_size("dp")
     row_count = lax.axis_size("row")
     col_count = lax.axis_size("col")
@@ -135,7 +151,7 @@
         D, 3 * width_col
     )
     w_out = lax.all_gather(output_weight, "row", axis=1, tiled=True)
-    w_gu = lax.all_gather(gate_up_weight, "row", axis=0, tiled=True).reshape(D, 2 * hidden_col)
+    w_gu = begin_bands_by_axis(gate_up_weight).reshape(D, 2 * hidden_col)
     w_down = lax.all_gather(down_weight, "row", axis=1, tiled=True)
 
     def to_tokens(values):

time: 1170 us -> 1260 us (1.077)
  other arithmetic: 66.5 us -> 112 us
  waiting for transfers between devices: 654 us -> 672 us
  starting transfers between devices: 16.8 us -> 29.5 us
    ppermute x0 -> x2, waiting for transfers between devices: none -> 198 us  [begin_bands_by_axis(): upper = lax.ppermute(aux, device_axis, f_next)]
    all_gather x1 -> x0, waiting for transfers between devices: 104 us -> none  [per_device(): lax.all_gather(gate_up_weight, 'row', axis=0, tiled=True)]
    all_gather x4, waiting for transfers between devices: 200 us -> 149 us  [gather_col(): return lax.all_gather(values, 'col', axis=0, tiled=True)]
    select_n x0 -> x3, other arithmetic: none -> 46.2 us  [begin_bands_by_axis(): aux = jnp.where(carry & x_next == 0, p_next, inter)]
    all_gather x1, waiting for transfers between devices: 20.5 us -> 0.01 us  [per_device(): w_down = lax.all_gather(down_weight, 'row', axis=1, tiled=True)]
    unnamed x173 -> x179, local copies, waits for them, and re-layouts: 41 us -> 49.8 us
    unnamed x17 -> x16, waiting for transfers between devices: 50.7 us -> 49.4 us
  transfers between devices with their start and end apart: 19 -> 20, of which waited for: 18 -> 16; matrix products, arithmetic and copies ran while one was open for 11% -> 16% of each run, Pallas kernels for 0% -> 0%
where the time goes in v1:
time: 1260 us; the launch traced here: 1250 us
  waiting for transfers between devices  672 us (53%)
  matrix products  217 us (17%)
  other arithmetic  112 us (9%)
  local copies, waits for them, and re-layouts  105 us (8%)
  blocking collectives  97.9 us (8%)
  starting transfers between devices  29.5 us (2%)
  between operations  16.9 us (1%)
    ppermute x2, waiting for transfers between devices, begin_bands_by_axis(): upper = lax.ppermute(aux, device_axis, f_next)  198 us
    reduce_scatter x4, waiting for transfers between devices, scatter_col(): lax.psum_scatter(values.astype(low), 'col', scatter_dimension=0, tiled=True)  172 us
    all_gather x4, waiting for transfers between devices, gather_col(): return lax.all_gather(values, 'col', axis=0, tiled=True)  149 us
    dot_general x18, matrix products, dot(): return jnp.dot(left, right, preferred_element_type=wide)  94 us
    dot_general x18, matrix products, dot_t(): return lax.dot_general(left, right, last_last, preferred_element_type=wide)  88.6 us
    unnamed x179, local copies, waits for them, and re-layouts  49.8 us
    unnamed x16, waiting for transfers between devices  49.4 us
    select_n x3, other arithmetic, begin_bands_by_axis(): aux = jnp.where(carry & x_next == 0, p_next, inter)  46.2 us
  transfers between devices with their start and end apart: 20, of which 16 were waited for; matrix products, arithmetic and copies ran while one was open for 16% of the time, Pallas kernels for 0%

profile of v1, /device:TPU:0, one launch (start us, length us, event | category | flops | bytes accessed | tf_op | source)
XLA Modules:
  0.0 1250.8 jit_solution(6102220294882803389)
XLA Ops:
  7.2 14.6 %all_to_all.84 = bf16[4,160,512]{2,1,0:T(8,128)(2,1)S(1)} all-to-all(bf16[4,160,512]{2,1,0:T(8,128)(2,1)} %bitcast.273), channel_id=1, replica_groups=mesh['dp'=2,'row'=4,'col'=4] {'row'}, dimensions={0} | all-to-all | bytes 1310720 | tf_op jit(solution)/shard_map/all_to_all | solution.py:158
  39.2 39.5 %all-gather.10.cloned.1.call-done = bf16[640,2048]{1,0:T(8,128)(2,1)} async-done(((bf16[160,2048]{1,0:T(8,128)(2,1)}), bf16[640,2048]{1,0:T(8,128)(2,1)}) %all-gather.10.cloned.1.call-update) | async-done | bytes 2621456 | tf_op jit(solution)/shard_map/all_gather | solution.py:164
  84.6 40.9 %all-gather.12.cloned.1.call-done = bf16[2048,3,512]{0,2,1:T(8,128)(2,1)} async-done(((bf16[512,3,512]{0,2,1:T(8,128)(2,1)}), bf16[2048,3,512]{0,2,1:T(8,128)(2,1)}) %all-gather.12.cloned.1.call-update) | async-done | bytes 6291472 | tf_op jit(solution)/shard_map/all_gather | solution.py:150
  136.8 12.0 psum.14
  178.9 34.2 %all-to-all-done.1 = bf16[4,640,384]{1,2,0:T(8,128)(2,1)} async-done(((bf16[4,640,384]{1,2,0:T(8,128)(2,1)}), bf16[4,640,384]{1,2,0:T(8,128)(2,1)}, u32[]{:S(2)}, u32[]{:S(2)}) %all-to-all-start.1) | async-done | bytes 1966112 | tf_op jit(solution)/shard_map/all_to_all | solution.py:177
  240.1 10.8 fusion.15
  251.0 12.7 %all_to_all.85 = bf16[4,640,128]{2,1,0:T(8,128)(2,1)S(1)} all-to-all(bf16[4,640,128]{2,1,0:T(8,128)(2,1)S(1)} %bitcast.257), channel_id=1, replica_groups=mesh['dp'=2,'row'=4,'col'=4] {'row'}, dimensions={0} | all-to-all | bytes 1310720 | tf_op jit(solution)/shard_map/all_to_all | solution.py:190
  279.5 41.4 %reduce-scatter.7.cloned.1.call-done = bf16[160,2048]{1,0:T(8,128)(2,1)} async-done(((bf16[640,2048]{1,0:T(8,128)(2,1)}), bf16[160,2048]{1,0:T(8,128)(2,1)}) %reduce-scatter.7.cloned.1.call-update) | async-done | bytes 655376 | tf_op jit(solution)/shard_map/reduce_scatter | solution.py:167
  324.6 21.1 %broadcast_select_fusion = bf16[1024,2,2048]{2,1,0:T(2,128)(2,1)} fusion(pred[]{:T(512)S(6)} %eq.94, bf16[512,2,2048]{2,1,0:T(2,128)(2,1)} %collective-permute-done, bf16[512,2,2048]{2,1,0:T(2,128)(2,1)} %param.34), kind=kLoop, calls=%fused_computation.7 | loop fusion | flops 12582912 | bytes 16777216 | tf_op jit(solution)/shard_map/jit(_where)/select_n | solution.py:108
  347.2 11.7 reduce-scatter.9.cloned.1.call-start
  375.3 197.7 %collective-permute-done.1 = bf16[1024,2,2048]{2,1,0:T(2,128)(2,1)} collective-permute-done((bf16[1024,2,2048]{2,1,0:T(2,128)(2,1)}, bf16[1024,2,2048]{2,1,0:T(2,128)(2,1)}, u32[]{:S(2)}, u32[]{:S(2)}) %collective-permute-start.1) | collective-permute-done | bytes 8388640 | tf_op jit(solution)/shard_map/ppermute | solution.py:105
  573.0 12.0 copy.135
  585.1 18.8 %maximum_select_fusion = bf16[2048,4096]{1,0:T(8,128)(2,1)} fusion(bf16[1024,4096]{1,0:T(8,128)(2,1)} %bitcast.227, bf16[1024,4096]{1,0:T(8,128)(2,1)} %maximum_select_fusion.1, pred[]{:T(512)S(6)} %eq.93), kind=kLoop, calls=%fused_computation.6 | loop fusion | flops 75497472 | bytes 33554432 | tf_op jit(solution)/shard_map/jit(_where)/select_n | solution.py:108
  612.8 11.6 fusion.23
  624.4 11.5 multiply_convert_fusion.3
  652.3 12.8 %all_to_all.86 = bf16[4,160,512]{2,1,0:T(8,128)(2,1)S(1)} all-to-all(bf16[4,160,512]{2,1,0:T(8,128)(2,1)S(1)} %bitcast.274), channel_id=1, replica_groups=mesh['dp'=2,'row'=4,'col'=4] {'row'}, dimensions={0} | all-to-all | bytes 1310720 | tf_op jit(solution)/shard_map/all_to_all | solution.py:158
  665.3 38.0 %reduce-scatter.9.cloned.1.call-done = bf16[160,2048]{1,0:T(8,128)(2,1)} async-done(((bf16[640,2048]{1,0:T(8,128)(2,1)}), bf16[160,2048]{1,0:T(8,128)(2,1)}) %reduce-scatter.9.cloned.1.call-update) | async-done | bytes 655376 | tf_op jit(solution)/shard_map/reduce_scatter | solution.py:167
  707.5 54.6 %all-gather.20.cloned.1.call-done = bf16[640,2048]{1,0:T(8,128)(2,1)} async-done(((bf16[160,2048]{1,0:T(8,128)(2,1)}), bf16[640,2048]{1,0:T(8,128)(2,1)}) %all-gather.20.cloned.1.call-update) | async-done | bytes 2621456 | tf_op jit(solution)/shard_map/all_gather | solution.py:164
  762.1 11.7 fusion.128
  775.4 10.0 multiply_convert_fusion.2
  798.0 11.3 add_convert_fusion.1
  809.3 51.0 %reduce-scatter.11.cloned.1.call-done = bf16[160,2048]{1,0:T(8,128)(2,1)} async-done(((bf16[640,2048]{1,0:T(8,128)(2,1)}), bf16[160,2048]{1,0:T(8,128)(2,1)}) %reduce-scatter.11.cloned.1.call-update) | async-done | bytes 655376 | tf_op jit(solution)/shard_map/reduce_scatter | solution.py:167
  864.9 54.6 %all-gather.22.cloned.1.call-done = bf16[640,2048]{1,0:T(8,128)(2,1)} async-done(((bf16[160,2048]{1,0:T(8,128)(2,1)}), bf16[640,2048]{1,0:T(8,128)(2,1)}) %all-gather.22.cloned.1.call-update) | async-done | bytes 2621456 | tf_op jit(solution)/shard_map/all_gather | solution.py:164
  927.1 13.0 %all_to_all.87 = bf16[4,640,128]{2,1,0:T(8,128)(2,1)S(1)} all-to-all(bf16[4,640,128]{2,1,0:T(8,128)(2,1)S(1)} %bitcast.259), channel_id=1, replica_groups=mesh['dp'=2,'row'=4,'col'=4] {'row'}, dimensions={0} | all-to-all | bytes 1310720 | tf_op jit(solution)/shard_map/all_to_all | solution.py:177
  940.2 11.3 fusion.20
  951.4 20.4 %multiply_reduce_fusion = (f32[2560]{0:T(1024)S(1)}, f32[2560,2560]{0,1:T(8,128)}) fusion(f32[2560]{0:T(1024)S(1)} %copy-done.62, f32[2560,2560]{0,1:T(8,128)} %copy-done.2, f32[2560]{0:T(1024)S(1)} %copy-done.60, bf16[2560,128]{1,0:T(8,128)(2,1)S(1)} %bitcast.276, bf16[2560,384]{1,0:T(8,128)(2,1)S(1)} %bitcast.252), kind=kOutput, calls=%fused_computation.1 | convolution fusion | flops 1703933440 | bytes 53774336 | tf_op jit(solution)/shard_map/dot_general | solution.py:23
  971.9 22.4 %multiply_convert_fusion = bf16[2560,2560]{0,1:T(8,128)(2,1)} fusion(f32[2560,2560]{0,1:T(8,128)} %get-tuple-element.100, f32[2560]{0:T(1024)S(1)} %get-tuple-element.99, f32[2560]{0:T(1024)S(1)} %copy-done.62, f32[2560,2560]{0,1:T(8,128)} %copy-done.2, f32[2560]{0:T(1024)S(1)} %copy-done.60), kind=kLoop, calls=%fused_computation | loop fusion | flops 32768000 | bytes 65566720 | tf_op jit(solution)/shard_map/convert_element_type | solution.py:278
  1026.0 17.8 %all-to-all-done.6 = bf16[4,640,384]{2,1,0:T(8,128)(2,1)S(1)} async-done(((bf16[4,640,384]{2,1,0:T(8,128)(2,1)}), bf16[4,640,384]{2,1,0:T(8,128)(2,1)S(1)}, u32[]{:S(2)}, u32[]{:S(2)}) %all-to-all-start.6) | async-done | bytes 1966112 | tf_op jit(solution)/shard_map/all_to_all | solution.py:190
  1064.6 9.6 psum.15
  1121.8 12.4 all-reduce.7.cloned.1.call-done
  1135.1 36.2 %all-reduce.5.cloned.1.call-done = bf16[4,7,4,512]{3,2,0,1:T(4,128)(2,1)} async-done(((bf16[4,7,4,512]{3,2,0,1:T(4,128)(2,1)}), bf16[4,7,4,512]{3,2,0,1:T(4,128)(2,1)}) %all-reduce.5.cloned.1.call-update) | async-done | bytes 114704
  1184.1 41.5 %reduce-scatter.13.cloned.1.call-done = bf16[160,2048]{1,0:T(8,128)(2,1)} async-done(((bf16[640,2048]{1,0:T(8,128)(2,1)}), bf16[160,2048]{1,0:T(8,128)(2,1)}) %reduce-scatter.13.cloned.1.call-update) | async-done | bytes 655376 | tf_op jit(solution)/shard_map/reduce_scatter | solution.py:167
  (359 shorter events, 314.7 us)
Async XLA Ops:
  7.2 357.3 %copy-start = (f32[2,8,16,2048]{3,2,1,0:T(8,128)S(1)}, f32[2,8,16,2048]{3,2,1,0:T(8,128)}, u32[]{:S(2)}) copy-start(f32[2,8,16,2048]{3,2,1,0:T(8,128)} %param.41) | copy-start | bytes 6291460
  7.2 71.5 %all-gather.10.cloned.1.call-start = ((), (), s32[]{:S(2)}) async-start(), calls=%async_computation.13 | async-start | bytes 3276800 | tf_op jit(solution)/shard_map/all_gather | solution.py:164
  22.8 102.7 %all-gather.12.cloned.1.call-start = ((), (), s32[]{:S(2)}) async-start(), calls=%async_computation.14 | async-start | bytes 7864320 | tf_op jit(solution)/shard_map/all_gather | solution.py:150
  36.0 46.7 %copy-start.32 = (bf16[3,16,2048]{2,1,0:T(8,128)(2,1)}, bf16[3,16,2048]{2,1,0:T(8,128)(2,1)S(1)}, u32[]{:S(2)}) copy-start(bf16[3,16,2048]{2,1,0:T(8,128)(2,1)S(1)} %slice.228) | copy-start | bytes 589828
  37.0 47.2 %copy-start.43 = (bf16[3,1,16,512]{3,2,1,0:T(8,128)(2,1)}, bf16[3,1,16,512]{3,2,1,0:T(8,128)(2,1)S(1)}, u32[]{:S(2)}) copy-start(bf16[3,1,16,512]{3,2,1,0:T(8,128)(2,1)S(1)} %dynamic-slice_convert_fusion.2) | copy-start | bytes 147460
  173.0 40.2 %all-to-all-start.1 = ((bf16[4,640,384]{1,2,0:T(8,128)(2,1)}), bf16[4,640,384]{1,2,0:T(8,128)(2,1)}, u32[]{:S(2)}, u32[]{:S(2)}) async-start(bf16[4,640,384]{1,2,0:T(8,128)(2,1)} %bitcast.245), calls=%async_computation.1 | async-start | bytes 3932160 | tf_op jit(solution)/shard_map/all_to_all | solution.py:177
  177.6 87.4 %all-gather.14.cloned.1.call-start = ((), (), s32[]{:S(2)}) async-start(), calls=%async_computation.15 | async-start | bytes 2621440 | tf_op jit(solution)/shard_map/all_gather | solution.py:153
  178.3 142.6 %reduce-scatter.7.cloned.1.call-start = ((), (), s32[]{:S(2)}) async-start(), calls=%async_computation.16 | async-start | bytes 3276800 | tf_op jit(solution)/shard_map/reduce_scatter | solution.py:167
  271.4 50.9 %copy-start.19 = (bf16[4,20,8,512]{3,2,0,1:T(8,128)(2,1)S(1)}, bf16[4,20,8,512]{3,2,0,1:T(8,128)(2,1)}, u32[]{:S(2)}) copy-start(bf16[4,20,8,512]{3,2,0,1:T(8,128)(2,1)} %copy.129) | copy-start | bytes 1966084
  271.4 332.4 %all-gather.16.cloned.1.call-start = ((), (), s32[]{:S(2)}) async-start(), calls=%async_computation.17 | async-start | bytes 3276800 | tf_op jit(solution)/shard_map/all_gather | solution.py:164
  271.5 53.1 %collective-permute-start = (bf16[512,2,2048]{2,1,0:T(2,128)(2,1)}, bf16[512,2,2048]{2,1,0:T(2,128)(2,1)}, u32[]{:S(2)}, u32[]{:S(2)}) collective-permute-start(bf16[512,2,2048]{2,1,0:T(2,128)(2,1)} %param.34), channel_id=1, source_target_pairs={{0,4},{4,0},{8,12},{12,8},{1,5},{5,1},{9,13},{13,9},{2,6},{6,2},{1... | collective-permute-start | bytes 12582920 | tf_op jit(solution)/shard_map/ppermute | solution.py:105
  324.5 314.6 %all-gather.18.cloned.1.call-start = ((), (), s32[]{:S(2)}) async-start(), calls=%async_computation.18 | async-start | bytes 10485760 | tf_op jit(solution)/shard_map/all_gather | solution.py:155
  345.7 227.3 %collective-permute-start.1 = (bf16[1024,2,2048]{2,1,0:T(2,128)(2,1)}, bf16[1024,2,2048]{2,1,0:T(2,128)(2,1)}, u32[]{:S(2)}, u32[]{:S(2)}) collective-permute-start(bf16[1024,2,2048]{2,1,0:T(2,128)(2,1)} %broadcast_select_fusion), channel_id=1, source_target_pairs={{0,8},{4,12},{8,0},{12,4},{1,9},{5,13},{9,1},{13,5},{2,10},{6,14},... | collective-permute-start | bytes 25165832 | tf_op jit(solution)/shard_map/ppermute | solution.py:105
  347.2 356.1 %reduce-scatter.9.cloned.1.call-start = ((), (), s32[]{:S(2)}) async-start(), calls=%async_computation.19 | async-start | bytes 3276800 | tf_op jit(solution)/shard_map/reduce_scatter | solution.py:167
  651.2 110.9 %all-gather.20.cloned.1.call-start = ((), (), s32[]{:S(2)}) async-start(), calls=%async_computation.20 | async-start | bytes 3276800 | tf_op jit(solution)/shard_map/all_gather | solution.py:164
  665.3 196.6 %copy-start.3 = (f32[4,20,8,512]{3,2,0,1:T(8,128)}, f32[4,20,8,512]{3,2,0,1:T(8,128)S(1)}, u32[]{:S(2)}) copy-start(f32[4,20,8,512]{3,2,0,1:T(8,128)S(1)} %copy.130) | copy-start | bytes 3932164
  707.4 152.9 %reduce-scatter.11.cloned.1.call-start = ((), (), s32[]{:S(2)}) async-start(), calls=%async_computation.21 | async-start | bytes 3276800 | tf_op jit(solution)/shard_map/reduce_scatter | solution.py:167
  762.1 24.1 %slice-start.4 = ((s8[16777216]{0:T(1024)(128)(4,1)}), s8[4194304]{0:T(1024)(128)(4,1)S(1)}, s32[]{:S(2)}) async-start(s8[16777216]{0:T(1024)(128)(4,1)} %bitcast.233), calls=%async_computation.31 | async-start | bytes 8388608
  762.1 24.1 %slice-start.5 = ((s8[16777216]{0:T(1024)(128)(4,1)}), s8[4194304]{0:T(1024)(128)(4,1)S(1)}, s32[]{:S(2)}) async-start(s8[16777216]{0:T(1024)(128)(4,1)} %bitcast.233), calls=%async_computation.32 | async-start | bytes 8388608
  762.1 24.2 %slice-start.6 = ((s8[16777216]{0:T(1024)(128)(4,1)}), s8[4194304]{0:T(1024)(128)(4,1)S(1)}, s32[]{:S(2)}) async-start(s8[16777216]{0:T(1024)(128)(4,1)} %bitcast.233), calls=%async_computation.33 | async-start | bytes 8388608
  809.3 51.1 %copy-start.20 = (bf16[160,2048]{1,0:T(8,128)(2,1)S(1)}, bf16[160,2048]{1,0:T(8,128)(2,1)}, u32[]{:S(2)}) copy-start(bf16[160,2048]{1,0:T(8,128)(2,1)} %reduce-scatter.7.cloned.1.call-done) | copy-start | bytes 1966084
  809.3 110.3 %all-gather.22.cloned.1.call-start = ((), (), s32[]{:S(2)}) async-start(), calls=%async_computation.22 | async-start | bytes 3276800 | tf_op jit(solution)/shard_map/all_gather | solution.py:164
  1015.7 28.0 %all-to-all-start.6 = ((bf16[4,640,384]{2,1,0:T(8,128)(2,1)}), bf16[4,640,384]{2,1,0:T(8,128)(2,1)S(1)}, u32[]{:S(2)}, u32[]{:S(2)}) async-start(bf16[4,640,384]{2,1,0:T(8,128)(2,1)} %bitcast.246), calls=%async_computation.9 | async-start | bytes 3932160 | tf_op jit(solution)/shard_map/all_to_all | solution.py:190
  1019.5 79.7 %reduce-scatter.15.cloned.1.call-start = ((), (), s32[]{:S(2)}) async-start(), calls=%async_computation.24 | async-start | bytes 573440 | tf_op jit(solution)/shard_map/reduce_scatter | solution.py:300
  1080.2 54.0 %all-reduce.7.cloned.1.call-start = ((), (), s32[]{:S(2)}) async-start(), calls=%async_computation.26 | async-start | bytes 524288
  1086.4 84.9 %all-reduce.5.cloned.1.call-start = ((), (), s32[]{:S(2)}) async-start(), calls=%async_computation.25 | async-start | bytes 229376
  1100.8 124.8 %reduce-scatter.13.cloned.1.call-start = ((), (), s32[]{:S(2)}) async-start(), calls=%async_computation.23 | async-start | bytes 3276800 | tf_op jit(solution)/shard_map/reduce_scatter | solution.py:167
  1107.7 14.1 %all-to-all-start.3 = ((bf16[160,4,512]{2,0,1:T(8,128)(2,1)}), bf16[160,4,512]{2,0,1:T(8,128)(2,1)S(1)}, u32[]{:S(2)}, u32[]{:S(2)}) async-start(bf16[160,4,512]{2,0,1:T(8,128)(2,1)} %bitcast.217), calls=%async_computation.5 | async-start | bytes 1310720 | tf_op jit(solution)/shard_map/all_to_all | solution.py:161
  1178.2 47.4 %copy-start.4 = (f32[4,20,8,512]{3,2,0,1:T(8,128)S(1)}, f32[4,20,8,512]{3,2,0,1:T(8,128)}, u32[]{:S(2)}) copy-start(f32[4,20,8,512]{3,2,0,1:T(8,128)} %copy-done.3) | copy-start | bytes 3932164
  1178.3 47.4 %copy-start.25 = (bf16[160,2048]{1,0:T(8,128)(2,1)S(1)}, bf16[160,2048]{1,0:T(8,128)(2,1)}, u32[]{:S(2)}) copy-start(bf16[160,2048]{1,0:T(8,128)(2,1)} %reduce-scatter.11.cloned.1.call-done) | copy-start | bytes 1966084
  1179.8 47.2 %copy-start.35 = (f32[4,7,4,512]{3,2,1,0:T(4,128)}, f32[4,7,4,512]{3,2,1,0:T(4,128)S(1)}, u32[]{:S(2)}) copy-start(f32[4,7,4,512]{3,2,1,0:T(4,128)S(1)} %reshape.353) | copy-start | bytes 688132
  1227.9 13.8 %all-to-all-start.7 = ((bf16[160,4,512]{2,0,1:T(8,128)(2,1)}), bf16[160,4,512]{2,0,1:T(8,128)(2,1)S(1)}, u32[]{:S(2)}, u32[]{:S(2)}) async-start(bf16[160,4,512]{2,0,1:T(8,128)(2,1)} %bitcast.216), calls=%async_computation.11 | async-start | bytes 1310720 | tf_op jit(solution)/shard_map/all_to_all | solution.py:161
  (70 other events, 415.6 us)
Sparse Core Ops, SparseCore 0:
  22.9 55.7 all-gather.9
  80.3 45.1 all-gather.11
  180.0 32.5 all-gather.13
  271.5 49.3 reduce-scatter.6
  324.6 54.4 all-gather.15
  380.6 102.1 all-gather.17
  651.3 51.9 reduce-scatter.8
  707.5 54.4 all-gather.19
  809.4 50.8 reduce-scatter.10
  865.0 54.4 all-gather.21
  1080.3 18.8 reduce-scatter.14
  1102.0 32.1 all-reduce.6
  1137.2 34.0 all-reduce.4
  1173.5 52.0 reduce-scatter.12
